TPU v7x, 32 devices: a whole 2x2x4 slice. The times are simulated.
32 devices in a mesh: dp: 8 (over z, x), mp: 4 (over y, core).
Axes of the slice: x: 2, y: 2, z: 4, core: 2. Of those that a mesh axis runs over, the one named last changes fastest.
Arguments:
- features: bfloat16 [8192, 1024], P('dp'), may hold values from -6 to 6
- out_grads: bfloat16 [8192, 4, 1024], P('dp', None, 'mp'), may hold values from -0.0625 to 0.0625
- norm_grads: float32 [8, 2048], P('dp'), may hold values from -2 to 2
- owners: int32 [5], replicated, may hold values from 0 to 7, as said below
- moment1: float32 [4, 1024, 1024], P(None, 'dp', 'mp'), may hold values from -6 to 6
- moment2: float32 [4, 1024, 1024], P(None, 'dp', 'mp'), may hold values from 0.1 to 10
- left_stats: float32 [4, 1024, 1024], P(None, 'dp', 'mp'), may hold values from -1024 to 1024, as said below
- right_stats: float32 [4, 1024, 1024], P(None, 'dp', 'mp'), may hold values from -1024 to 1024, as said below
- left_basis: float32 [4, 1024, 1024], P(None, 'dp', 'mp'), may hold values from -1 to 2
- right_basis: float32 [4, 1024, 1024], P(None, 'dp', 'mp'), may hold values from -1 to 2
- norm_m: float32 [2048], P('dp'), may hold values from -6 to 6
- norm_v: float32 [2048], P('dp'), may hold values from 0.1 to 10
Outputs:
- new_moment1: float32 [4, 1024, 1024], P(None, 'dp', 'mp')
- new_moment2: float32 [4, 1024, 1024], P(None, 'dp', 'mp')
- new_left_stats: float32 [4, 1024, 1024], P(None, 'dp', 'mp')
- new_right_stats: float32 [4, 1024, 1024], P(None, 'dp', 'mp')
- new_left_basis: float32 [4, 1024, 1024], P(None, 'dp', 'mp')
- new_right_basis: float32 [4, 1024, 1024], P(None, 'dp', 'mp')
- update_slots: bfloat16 [8, 1024, 1024], P('dp', None, 'mp')
- new_norm_m: float32 [2048], P('dp')
- new_norm_v: float32 [2048], P('dp')
- norm_slots: float32 [8, 2048], P('dp')
Inputs may be any that keep to these rules, and one draw needn't show every extreme that they name: `owners`: the first 4 entries are distinct, so a dp index owns at most one tile; the last entry may equal any of them. `left_stats`: each tile of statistics is symmetric. `right_stats`: each tile of statistics is symmetric.
All inputs are finite; a program needn't handle non-finite values.
Results may differ from a plain program's by a relative error of at most 0.0072.
Values may be sent and summed in bfloat16 or wider, within the bound.
A program may use at most 128 MiB of HBM per device.

v0:
```python
import jax
import jax.numpy as jnp
from jax import lax
from jax.sharding import PartitionSpec as P

FIX_ONE = 1.0 - 0.9**10
FIX_TWO = 1.0 - 0.95**10
BF = jnp.bfloat16
F32 = jnp.float32


def contract(left, right, left_dim, right_dim):
    return lax.dot_general(
        left, right, (((left_dim,), (right_dim,)), ((), ())), preferred_element_type=F32
    )


def to_tile(blocks):
    out = lax.all_to_all(blocks, "mp", split_axis=1, concat_axis=1, tiled=True)
    k, n, r, c = out.shape
    return out.transpose(0, 2, 1, 3).reshape(k, r, n * c)


def to_home(rows, n):
    k, r, c = rows.shape
    out = rows.reshape(k, r, n, c // n).transpose(0, 2, 1, 3)
    return lax.all_to_all(out, "mp", split_axis=1, concat_axis=1, tiled=True)


def gather_rows(rows):
    return lax.all_gather(rows, "dp", axis=0, tiled=True)


def normalize(power):
    wide = power.astype(F32)
    return lax.rsqrt(jnp.sum(wide * wide, axis=0, keepdims=True) + 1e-06)


def shards(
    features,
    out_grads,
    norm_grads,
    owners,
    moment1,
    moment2,
    left_stats,
    right_stats,
    left_basis,
    right_basis,
    norm_m,
    norm_v,
):
    dp = lax.axis_size("dp")
    tiles, slab, width = moment1.shape
    full = slab * dp
    me = lax.axis_index("dp")
    row0 = me * slab
    narrow = to_tile(jnp.stack([left_basis, right_basis, left_stats, right_stats]).astype(BF))
    left_full = gather_rows(narrow[0])
    right_full = gather_rows(narrow[1])
    flat = out_grads.reshape(out_grads.shape[0], tiles * width)
    partial = contract(features, flat, 0, 0).astype(BF).reshape(dp, slab, tiles * width)
    parts = lax.all_to_all(partial, "dp", split_axis=0, concat_axis=0, tiled=True)
    grad_home = jnp.sum(parts.astype(F32), axis=0).astype(BF)
    grad_home = grad_home.reshape(slab, tiles, width).transpose(1, 0, 2)
    grad_rows = to_tile(grad_home[None])[0]
    grad_full = gather_rows(grad_rows)
    wide = to_tile(jnp.stack([moment1, moment2]))
    prod_l = contract(grad_rows, grad_full, 1, 1)
    grad_cols = lax.dynamic_slice_in_dim(grad_full, row0, slab, 1)
    prod_r = contract(grad_cols, grad_full, 0, 0)
    stats_l = (0.95 * narrow[2].astype(F32) + 0.05 * prod_l).astype(BF)
    stats_r = (0.95 * narrow[3].astype(F32) + 0.05 * prod_r).astype(BF)
    power_l = contract(stats_l, left_full, 1, 0).astype(BF)
    power_r = contract(stats_r, right_full, 1, 0).astype(BF)
    power_l_full = gather_rows(power_l)
    power_r_full = gather_rows(power_r)
    left_cols = lax.dynamic_slice_in_dim(left_full, row0, slab, 1)
    half = contract(left_cols, grad_full, 0, 0).astype(BF)
    rotated = contract(half, right_full, 1, 0)
    tile_one = 0.9 * wide[0] + 0.1 * rotated
    tile_two = 0.95 * wide[1] + 0.05 * rotated * rotated
    direction = (tile_one / FIX_ONE / (jnp.sqrt(tile_two / FIX_TWO) + 1e-08)).astype(BF)
    back = contract(direction, right_full, 1, 1).astype(BF)
    back_full = gather_rows(back)
    home1 = to_home(jnp.stack([rotated, prod_l, prod_r]).astype(BF), tiles).astype(F32)
    new_one = 0.9 * moment1 + 0.1 * home1[0]
    new_two = 0.95 * moment2 + 0.05 * home1[0] * home1[0]
    new_sl = 0.95 * left_stats + 0.05 * home1[1]
    new_sr = 0.95 * right_stats + 0.05 * home1[2]
    update = contract(narrow[0], back_full, 1, 0).astype(BF)

    def refine(power_full, power_rows):
        scale = normalize(power_full)
        iter_full = (power_full.astype(F32) * scale).astype(BF)
        iter_rows = (power_rows.astype(F32) * scale).astype(BF)
        gram = contract(iter_rows, iter_full, 1, 1).astype(BF)
        return 1.5 * iter_rows.astype(F32) - 0.5 * contract(gram, iter_full, 1, 0)

    new_l = refine(power_l_full, power_l)
    new_r = refine(power_r_full, power_r)
    home2 = to_home(jnp.stack([new_l.astype(BF), new_r.astype(BF), update]), tiles)
    new_bl = home2[0].astype(F32)
    new_br = home2[1].astype(F32)
    slot_of = jnp.arange(dp, dtype=jnp.int32)[:, None, None]
    slots = jnp.zeros((dp, slab, width), BF)
    for n in range(tiles):
        slots = jnp.where(slot_of == owners[n], home2[2, n][None], slots)
    update_slot = lax.all_to_all(slots, "dp", split_axis=0, concat_axis=0, tiled=True)
    update_slot = update_slot.reshape(1, full, width)
    norm_parts = norm_grads.reshape(dp, norm_m.shape[0])
    norm_parts = lax.all_to_all(norm_parts, "dp", split_axis=0, concat_axis=0, tiled=True)
    norm_total = jnp.sum(norm_parts, axis=0)
    new_nm = 0.9 * norm_m + 0.1 * norm_total
    new_nv = 0.95 * norm_v + 0.05 * norm_total * norm_total
    norm_step = new_nm / FIX_ONE / (jnp.sqrt(new_nv / FIX_TWO) + 1e-08)
    to_owner = (jnp.arange(dp, dtype=jnp.int32) == owners[tiles])[:, None]
    norm_out = jnp.where(to_owner, norm_step[None], 0.0)
    norm_slot = lax.all_to_all(norm_out, "dp", split_axis=0, concat_axis=0, tiled=True)
    norm_slot = norm_slot.reshape(1, -1)
    return (
        new_one,
        new_two,
        new_sl,
        new_sr,
        new_bl,
        new_br,
        update_slot,
        new_nm,
        new_nv,
        norm_slot,
    )


def solution(mesh):
    in_specs = (
        P("dp", None),
        P("dp", None, "mp"),
        P("dp", None),
        P(),
        P(None, "dp", "mp"),
        P(None, "dp", "mp"),
        P(None, "dp", "mp"),
        P(None, "dp", "mp"),
        P(None, "dp", "mp"),
        P(None, "dp", "mp"),
        P("dp"),
        P("dp"),
    )
    out_specs = (
        P(None, "dp", "mp"),
        P(None, "dp", "mp"),
        P(None, "dp", "mp"),
        P(None, "dp", "mp"),
        P(None, "dp", "mp"),
        P(None, "dp", "mp"),
        P("dp", None, "mp"),
        P("dp"),
        P("dp"),
        P("dp", None),
    )
    return jax.shard_map(shards, mesh=mesh, in_specs=in_specs, out_specs=out_specs, check_vma=False)
```

profile of v0, /device:TPU:0, one launch (start us, length us, event | category | flops | bytes accessed | tf_op | source)
XLA Modules:
  0.0 443.4 jit_solution(10692234722072050169)
XLA Ops:
  7.2 2.2 copy.122
  9.5 2.4 convolution_convert_fusion
  11.9 55.4 %all_to_all.50 = bf16[8,128,1024]{2,1,0:T(8,128)(2,1)} all-to-all(bf16[8,128,1024]{2,1,0:T(8,128)(2,1)S(1)} %bitcast.115), channel_id=1, replica_groups=mesh['dp'=8,'mp'=4] {'dp'}, dimensions={0} | all-to-all | bytes 4194304 | tf_op jit(solution)/shard_map/all_to_all | solution.py:63
  67.3 2.0 reduce_sum.39
  69.4 0.8 copy.97
  70.2 1.1 copy.98
  71.3 9.1 %all_to_all.51 = bf16[1,4,128,256]{3,2,0,1:T(8,128)(2,1)} all-to-all(bf16[1,4,128,256]{3,2,0,1:T(8,128)(2,1)S(1)} %copy.98), channel_id=1, replica_groups=mesh['dp'=8,'mp'=4] {'mp'}, dimensions={1} | all-to-all | bytes 524288 | tf_op jit(solution)/shard_map/all_to_all | solution.py:19
  80.4 1.8 copy.99
  82.6 1.2 copy.93
  83.8 1.2 copy.92
  85.2 16.9 %all_to_all.52 = bf16[4,4,128,256]{2,3,0,1:T(8,128)(2,1)S(1)} all-to-all(bf16[4,4,128,256]{2,3,0,1:T(8,128)(2,1)S(1)} %pad_maximum_fusion), channel_id=1, replica_groups=mesh['dp'=8,'mp'=4] {'mp'}, dimensions={1} | all-to-all | bytes 2097152 | tf_op jit(solution)/shard_map/all_to_all | solution.py:19
  102.1 0.8 fusion.83
  103.0 0.7 all-gather.7.cloned.1.call-update
  103.8 1.1 convert_multiply_fusion.5
  104.8 1.2 copy.117
  106.1 24.6 %all-gather.9.cloned.1.call-done = bf16[1024,1024]{0,1:T(8,128)(2,1)} async-done(((bf16[128,1024]{0,1:T(8,128)(2,1)}), bf16[1024,1024]{0,1:T(8,128)(2,1)}) %all-gather.9.cloned.1.call-update) | async-done | bytes 2097168 | tf_op jit(solution)/shard_map/all_gather | solution.py:31
  130.7 3.4 fusion.85
  134.1 47.8 %all-gather.11.cloned.1.call-done = bf16[1024,1024]{0,1:T(8,128)(2,1)} async-done(((bf16[128,1024]{0,1:T(8,128)(2,1)}), bf16[1024,1024]{0,1:T(8,128)(2,1)}) %all-gather.11.cloned.1.call-update) | async-done | bytes 2097168 | tf_op jit(solution)/shard_map/all_gather | solution.py:31
  181.8 3.3 convolution_convert_fusion.3
  185.3 0.2 copy.116
  185.5 2.8 fusion.86
  188.2 44.8 %all-gather.7.cloned.1.call-done = bf16[1024,1024]{0,1:T(8,128)(2,1)} async-done(((bf16[128,1024]{0,1:T(8,128)(2,1)}), bf16[1024,1024]{0,1:T(8,128)(2,1)}) %all-gather.7.cloned.1.call-update) | async-done | bytes 2097168 | tf_op jit(solution)/shard_map/all_gather | solution.py:31
  233.0 3.1 convolution_convert_fusion.4
  236.2 1.2 copy.108
  237.4 1.2 copy.109
  238.8 17.0 %all_to_all.53 = f32[2,4,128,256]{2,3,0,1:T(8,128)S(1)} all-to-all(f32[2,4,128,256]{2,3,0,1:T(8,128)S(1)} %pad_maximum_fusion.1), channel_id=1, replica_groups=mesh['dp'=8,'mp'=4] {'mp'}, dimensions={1} | all-to-all | bytes 2097152 | tf_op jit(solution)/shard_map/all_to_all | solution.py:19
  255.9 1.0 copy.118
  257.1 4.8 %fusion.87 = (bf16[128,1024]{1,0:T(8,128)(2,1)}, f32[128,1024]{1,0:T(8,128)}) fusion(bf16[1024,1024]{0,1:T(8,128)(2,1)} %all-gather.11.cloned.1.call-done, bf16[1024,1024]{0,1:T(8,128)(2,1)} %all-gather.9.cloned.1.call-done, bf16[1024,1024]{0,1:T(8,128)(2,1)} %all-gather.7.cloned.1.call-done, s32[]{:T(128)S(6)} %select_n.28), kind=kOutput, calls=%fused_computation.109 | convolution fusion | flops 537133056 | bytes 5242884 | tf_op jit(solution)/shard_map/dot_general | solution.py:13
  261.9 3.1 convolution_convert_fusion.2
  265.1 3.5 all-to-all-start.7
  268.6 0.7 fusion.84
  269.3 0.7 iota_compare_fusion
  269.9 5.2 %all-to-all-done.7 = f32[8,1,256]{2,1,0:T(1,128)S(1)} async-done(((f32[8,1,256]{2,1,0:T(1,128)}), f32[8,1,256]{2,1,0:T(1,128)S(1)}, u32[]{:S(2)}, u32[]{:S(2)}) %all-to-all-start.7) | async-done | bytes 8224 | tf_op jit(solution)/shard_map/all_to_all | solution.py:112
  275.2 0.6 add_divide_fusion
  275.8 0.7 broadcast_select_fusion
  276.4 3.5 all-to-all-start.8
  280.0 3.1 all-gather.15.cloned.1.call-done
  283.1 2.1 fusion.2
  285.1 3.5 fusion.24
  288.9 43.8 %all-gather.13.cloned.1.call-done = bf16[1024,1024]{1,0:T(8,128)(2,1)} async-done(((bf16[128,1024]{1,0:T(8,128)(2,1)}), bf16[1024,1024]{1,0:T(8,128)(2,1)}) %all-gather.13.cloned.1.call-update) | async-done | bytes 2097168 | tf_op jit(solution)/shard_map/all_gather | solution.py:31
  332.7 2.1 fusion
  334.8 3.5 fusion.27
  338.5 44.4 %all-gather.17.cloned.1.call-done = bf16[1024,1024]{1,0:T(8,128)(2,1)} async-done(((bf16[128,1024]{1,0:T(8,128)(2,1)}), bf16[1024,1024]{1,0:T(8,128)(2,1)}) %all-gather.17.cloned.1.call-update) | async-done | bytes 2097168 | tf_op jit(solution)/shard_map/all_gather | solution.py:31
  382.9 2.1 convolution_convert_fusion.1
  385.2 1.0 maximum_bitcast_fusion.1
  386.2 3.6 all-to-all-start.5
  389.8 1.8 stack.58
  391.6 1.7 copy.100
  393.3 0.9 stack.60
  394.2 1.7 copy.102
  396.1 2.0 maximum_bitcast_fusion
  398.1 3.3 all-to-all-done.5
  401.4 4.2 all-to-all-start.3
  405.6 1.3 iota_compare_fusion.1
  406.9 1.2 iota_compare_fusion.3
  408.1 1.1 select_select_fusion
  409.2 8.1 %all-to-all-done.3 = bf16[3,4,128,256]{3,2,0,1:T(8,128)(2,1)} async-done(((bf16[3,4,128,256]{3,2,0,1:T(8,128)(2,1)}), bf16[3,4,128,256]{3,2,0,1:T(8,128)(2,1)}, u32[]{:S(2)}, u32[]{:S(2)}) %all-to-all-start.3) | async-done | bytes 786464 | tf_op jit(solution)/shard_map/all_to_all | solution.py:27
  417.3 3.5 all-to-all-start.6
  420.8 1.4 convert_element_type.101
  422.5 1.5 fusion.48
  424.0 1.1 fusion.54
  425.1 10.1 %all-to-all-done.6 = bf16[8,128,256]{2,1,0:T(8,128)(2,1)S(1)} async-done(((bf16[8,128,256]{2,1,0:T(8,128)(2,1)}), bf16[8,128,256]{2,1,0:T(8,128)(2,1)S(1)}, u32[]{:S(2)}, u32[]{:S(2)}) %all-to-all-start.6) | async-done | bytes 524320 | tf_op jit(solution)/shard_map/all_to_all | solution.py:109
  435.1 0.8 copy.129
  435.9 0.6 copy.130
  (68 shorter events, 2.6 us)
Async XLA Ops:
  7.2 2.3 copy-start
  7.2 123.5 %all-gather.9.cloned.1.call-start = ((), (), s32[]{:S(2)}) async-start(), calls=%async_computation.10 | async-start | bytes 2359296 | tf_op jit(solution)/shard_map/all_gather | solution.py:31
  67.3 14.9 %copy-start.4 = (f32[4,128,256]{2,1,0:T(8,128)S(1)}, f32[4,128,256]{2,1,0:T(8,128)}, u32[]{:S(2)}) copy-start(f32[4,128,256]{2,1,0:T(8,128)} %param.19) | copy-start | bytes 1572868
  69.3 13.1 %copy-start.6 = (f32[4,128,256]{2,1,0:T(8,128)S(1)}, f32[4,128,256]{2,1,0:T(8,128)}, u32[]{:S(2)}) copy-start(f32[4,128,256]{2,1,0:T(8,128)} %param.18) | copy-start | bytes 1572868
  82.2 99.7 %all-gather.11.cloned.1.call-start = ((), (), s32[]{:S(2)}) async-start(), calls=%async_computation.11 | async-start | bytes 2359296 | tf_op jit(solution)/shard_map/all_gather | solution.py:31
  103.0 130.1 %all-gather.7.cloned.1.call-start = ((), (), s32[]{:S(2)}) async-start(), calls=%async_computation.9 | async-start | bytes 2359296 | tf_op jit(solution)/shard_map/all_gather | solution.py:31
  103.7 179.4 %all-gather.15.cloned.1.call-start = ((), (), s32[]{:S(2)}) async-start(), calls=%async_computation.13 | async-start | bytes 2359296 | tf_op jit(solution)/shard_map/all_gather | solution.py:31
  134.0 51.2 %copy-start.3 = (f32[1,128,4,256]{1,3,2,0:T(8,128)S(1)}, f32[1,128,4,256]{1,3,2,0:T(8,128)}, u32[]{:S(2)}) copy-start(f32[1,128,4,256]{1,3,2,0:T(8,128)} %get-tuple-element.17) | copy-start | bytes 1572868
  181.8 3.6 copy-start.1
  185.2 147.5 %all-gather.13.cloned.1.call-start = ((), (), s32[]{:S(2)}) async-start(), calls=%async_computation.12 | async-start | bytes 2359296 | tf_op jit(solution)/shard_map/all_gather | solution.py:31
  236.2 146.7 %all-gather.17.cloned.1.call-start = ((), (), s32[]{:S(2)}) async-start(), calls=%async_computation.14 | async-start | bytes 2359296 | tf_op jit(solution)/shard_map/all_gather | solution.py:31
  257.1 4.8 %copy-start.14 = (f32[128,1024]{1,0:T(8,128)S(1)}, f32[128,1024]{1,0:T(8,128)}, u32[]{:S(2)}) copy-start(f32[128,1024]{1,0:T(8,128)} %copy.118) | copy-start | bytes 1572868
  261.9 6.7 %copy-start.15 = (s32[5]{0:T(128)S(1)}, s32[5]{0:T(128)}, u32[]{:S(2)}) copy-start(s32[5]{0:T(128)} %param.15) | copy-start | bytes 64
  261.9 13.3 %copy-start.16 = (f32[256]{0:T(256)S(1)}, f32[256]{0:T(256)}, u32[]{:S(2)}) copy-start(f32[256]{0:T(256)} %param.23) | copy-start | bytes 3076
  261.9 13.3 %copy-start.17 = (f32[256]{0:T(256)S(1)}, f32[256]{0:T(256)}, u32[]{:S(2)}) copy-start(f32[256]{0:T(256)} %param.22) | copy-start | bytes 3076
  265.1 20.1 %copy-start.12 = (bf16[128,1024]{1,0:T(8,128)(2,1)S(1)}, bf16[128,1024]{1,0:T(8,128)(2,1)}, u32[]{:S(2)}) copy-start(bf16[128,1024]{1,0:T(8,128)(2,1)} %convolution_convert_fusion.3) | copy-start | bytes 786436
  265.1 10.1 %all-to-all-start.7 = ((f32[8,1,256]{2,1,0:T(1,128)}), f32[8,1,256]{2,1,0:T(1,128)S(1)}, u32[]{:S(2)}, u32[]{:S(2)}) async-start(f32[8,1,256]{2,1,0:T(1,128)} %bitcast.38), calls=%async_computation.7 | async-start | bytes 16384 | tf_op jit(solution)/shard_map/all_to_all | solution.py:112
  276.4 109.7 %all-to-all-start.8 = ((f32[8,1,256]{2,1,0:T(1,128)}), f32[8,1,256]{2,1,0:T(1,128)S(1)}, u32[]{:S(2)}, u32[]{:S(2)}) async-start(f32[8,1,256]{2,1,0:T(1,128)} %broadcast_select_fusion), calls=%async_computation.8 | async-start | bytes 16384 | tf_op jit(solution)/shard_map/all_to_all | solution.py:119
  288.6 46.1 %copy-start.13 = (bf16[128,1024]{1,0:T(8,128)(2,1)S(1)}, bf16[128,1024]{1,0:T(8,128)(2,1)}, u32[]{:S(2)}) copy-start(bf16[128,1024]{1,0:T(8,128)(2,1)} %convolution_convert_fusion.4) | copy-start | bytes 786436
  334.7 48.1 %copy-start.2 = (bf16[1,128,4,256]{1,3,2,0:T(8,128)(2,1)S(1)}, bf16[1,128,4,256]{1,3,2,0:T(8,128)(2,1)}, u32[]{:S(2)}) copy-start(bf16[1,128,4,256]{1,3,2,0:T(8,128)(2,1)} %get-tuple-element.21) | copy-start | bytes 786436
  385.2 8.2 %copy-start.10 = (bf16[128,1024]{1,0:T(8,128)(2,1)S(1)}, bf16[128,1024]{1,0:T(8,128)(2,1)}, u32[]{:S(2)}) copy-start(bf16[128,1024]{1,0:T(8,128)(2,1)} %get-tuple-element.34) | copy-start | bytes 786436
  386.2 9.7 %copy-start.11 = (bf16[128,1024]{1,0:T(8,128)(2,1)S(1)}, bf16[128,1024]{1,0:T(8,128)(2,1)}, u32[]{:S(2)}) copy-start(bf16[128,1024]{1,0:T(8,128)(2,1)} %get-tuple-element.36) | copy-start | bytes 786436
  386.2 15.2 %all-to-all-start.5 = ((bf16[3,4,128,256]{3,2,0,1:T(8,128)(2,1)}), bf16[3,4,128,256]{3,2,0,1:T(8,128)(2,1)S(1)}, u32[]{:S(2)}, u32[]{:S(2)}) async-start(bf16[3,4,128,256]{3,2,0,1:T(8,128)(2,1)} %maximum_bitcast_fusion.1), calls=%async_computation.5 | async-start | bytes 1572864 | tf_op jit(solution)/shard_map/all_to_all | solution.py:27
  401.4 15.9 %all-to-all-start.3 = ((bf16[3,4,128,256]{3,2,0,1:T(8,128)(2,1)}), bf16[3,4,128,256]{3,2,0,1:T(8,128)(2,1)}, u32[]{:S(2)}, u32[]{:S(2)}) async-start(bf16[3,4,128,256]{3,2,0,1:T(8,128)(2,1)} %maximum_bitcast_fusion), calls=%async_computation.3 | async-start | bytes 1572864 | tf_op jit(solution)/shard_map/all_to_all | solution.py:27
  417.3 17.9 %all-to-all-start.6 = ((bf16[8,128,256]{2,1,0:T(8,128)(2,1)}), bf16[8,128,256]{2,1,0:T(8,128)(2,1)S(1)}, u32[]{:S(2)}, u32[]{:S(2)}) async-start(bf16[8,128,256]{2,1,0:T(8,128)(2,1)} %select_select_fusion), calls=%async_computation.6 | async-start | bytes 1048576 | tf_op jit(solution)/shard_map/all_to_all | solution.py:109
  420.8 1.5 copy-start.5
  420.8 1.5 copy-start.7
  420.8 1.6 copy-start.8
  420.8 1.7 copy-start.9
Sparse Core Ops, SparseCore 0:
  82.3 48.3 all-gather.8
  133.3 48.5 all-gather.10
  184.5 48.5 all-gather.6
  235.6 47.4 all-gather.14
  285.0 47.5 all-gather.12
  335.2 47.6 all-gather.16
where the time goes:
time: 445 us; the launch traced here: 443 us
  waiting for transfers between devices  236 us (53%)
  blocking collectives  98.3 us (22%)
  matrix products  32 us (7%)
  local copies, waits for them, and re-layouts  24.2 us (5%)
  other arithmetic  20 us (4%)
  starting transfers between devices  18.5 us (4%)
  between operations  14.6 us (3%)
    all_gather x6, waiting for transfers between devices, gather_rows(): return lax.all_gather(rows, 'dp', axis=0, tiled=True)  208 us
    all_to_all x1, blocking collectives, shards(): lax.all_to_all(partial, 'dp', split_axis=0, concat_axis=0, tiled=True)  55.4 us
    all_to_all x3, blocking collectives, to_tile(): out = lax.all_to_all(blocks, 'mp', split_axis=1, concat_axis=1, tiled=True)  42.9 us
    dot_general x10, matrix products, contract(): lax.dot_general(left, right, (((left_dim,), (right_dim,)), ((), ())), pre...  32 us
    all_to_all x2, waiting for transfers between devices, to_home(): return lax.all_to_all(out, 'mp', split_axis=1, concat_axis=1, tiled=True)  11.3 us
    all_to_all x1, waiting for transfers between devices, shards(): lax.all_to_all(slots, 'dp', split_axis=0, concat_axis=0, tiled=True)  10.1 us
    unnamed x45, local copies, waits for them, and re-layouts  9.22 us
  transfers between devices with their start and end apart: 11, of which 10 were waited for; matrix products, arithmetic and copies ran while one was open for 14% of the time, Pallas kernels for 0%

commit v1 on v0

--- a/solution.py
+++ b/solution.py
@@ -24,7 +24,9 @@
 def to_home(rows, n):
     k, r, c = rows.shape
     out = rows.reshape(k, r, n, c // n).transpose(0, 2, 1, 3)
-    return lax.all_to_all(out, "mp", split_axis=1, concat_axis=1, tiled=True)
+    return jnp.concatenate(
+        lax.all_to_all(jnp.stack(jnp.split(out, lax.axis_size("mp"), axis=1)), "mp", 0, 0), axis=1
+    )
 
 
 def gather_rows(rows):

time: 445 us -> 445 us (level)
  transfers between devices with their start and end apart: 11 -> 11, of which waited for: 10 -> 10; matrix products, arithmetic and copies ran while one was open for 14% -> 15% of each run, Pallas kernels for 0% -> 0%
where the time goes in v1:
time: 445 us; the launch traced here: 444 us
  waiting for transfers between devices  236 us (53%)
  blocking collectives  98.3 us (22%)
  matrix products  31.9 us (7%)
  local copies, waits for them, and re-layouts  24.3 us (5%)
  other arithmetic  20.3 us (5%)
  starting transfers between devices  18.5 us (4%)
  between operations  14.6 us (3%)
    all_gather x6, waiting for transfers between devices, gather_rows(): return lax.all_gather(rows, 'dp', axis=0, tiled=True)  208 us
    all_to_all x1, blocking collectives, shards(): lax.all_to_all(partial, 'dp', split_axis=0, concat_axis=0, tiled=True)  55.4 us
    all_to_all x3, blocking collectives, to_tile(): out = lax.all_to_all(blocks, 'mp', split_axis=1, concat_axis=1, tiled=True)  42.9 us
    dot_general x10, matrix products, contract(): lax.dot_general(left, right, (((left_dim,), (right_dim,)), ((), ())), pre...  31.9 us
    all_to_all x2, waiting for transfers between devices, to_home(): lax.all_to_all(jnp.stack(jnp.split(out, lax.axis_size('mp'), axis=1)), 'm...  11 us
    all_to_all x1, waiting for transfers between devices, shards(): lax.all_to_all(slots, 'dp', split_axis=0, concat_axis=0, tiled=True)  10.1 us
    unnamed x45, local copies, waits for them, and re-layouts  9.22 us
  transfers between devices with their start and end apart: 11, of which 10 were waited for; matrix products, arithmetic and copies ran while one was open for 15% of the time, Pallas kernels for 0%

profile of v1, /device:TPU:0, one launch (start us, length us, event | category | flops | bytes accessed | tf_op | source)
XLA Modules:
  0.0 443.6 jit_solution(13945843990971652355)
XLA Ops:
  7.2 2.2 copy.152
  9.5 2.4 convolution_convert_fusion
  11.9 55.4 %all_to_all.50 = bf16[8,128,1024]{2,1,0:T(8,128)(2,1)} all-to-all(bf16[8,128,1024]{2,1,0:T(8,128)(2,1)S(1)} %bitcast.150), channel_id=1, replica_groups=mesh['dp'=8,'mp'=4] {'dp'}, dimensions={0} | all-to-all | bytes 4194304 | tf_op jit(solution)/shard_map/all_to_all | solution.py:65
  67.3 2.0 reduce_sum.39
  69.4 0.8 copy.121
  70.2 1.1 copy.122
  71.3 9.1 %all_to_all.51 = bf16[1,4,128,256]{3,2,0,1:T(8,128)(2,1)} all-to-all(bf16[1,4,128,256]{3,2,0,1:T(8,128)(2,1)S(1)} %copy.122), channel_id=1, replica_groups=mesh['dp'=8,'mp'=4] {'mp'}, dimensions={1} | all-to-all | bytes 524288 | tf_op jit(solution)/shard_map/all_to_all | solution.py:19
  80.4 1.8 copy.123
  82.6 1.2 copy.117
  83.8 1.2 copy.116
  85.2 16.9 %all_to_all.52 = bf16[4,4,128,256]{2,3,0,1:T(8,128)(2,1)S(1)} all-to-all(bf16[4,4,128,256]{2,3,0,1:T(8,128)(2,1)S(1)} %pad_maximum_fusion), channel_id=1, replica_groups=mesh['dp'=8,'mp'=4] {'mp'}, dimensions={1} | all-to-all | bytes 2097152 | tf_op jit(solution)/shard_map/all_to_all | solution.py:19
  102.1 0.8 fusion.83
  103.0 0.7 all-gather.7.cloned.1.call-update
  103.8 1.1 convert_multiply_fusion.5
  104.8 1.2 copy.147
  106.1 24.6 %all-gather.9.cloned.1.call-done = bf16[1024,1024]{0,1:T(8,128)(2,1)} async-done(((bf16[128,1024]{0,1:T(8,128)(2,1)}), bf16[1024,1024]{0,1:T(8,128)(2,1)}) %all-gather.9.cloned.1.call-update) | async-done | bytes 2097168 | tf_op jit(solution)/shard_map/all_gather | solution.py:33
  130.7 3.4 fusion.85
  134.1 47.8 %all-gather.11.cloned.1.call-done = bf16[1024,1024]{0,1:T(8,128)(2,1)} async-done(((bf16[128,1024]{0,1:T(8,128)(2,1)}), bf16[1024,1024]{0,1:T(8,128)(2,1)}) %all-gather.11.cloned.1.call-update) | async-done | bytes 2097168 | tf_op jit(solution)/shard_map/all_gather | solution.py:33
  181.8 3.3 convolution_convert_fusion.3
  185.5 2.8 fusion.86
  188.2 44.8 %all-gather.7.cloned.1.call-done = bf16[1024,1024]{0,1:T(8,128)(2,1)} async-done(((bf16[128,1024]{0,1:T(8,128)(2,1)}), bf16[1024,1024]{0,1:T(8,128)(2,1)}) %all-gather.7.cloned.1.call-update) | async-done | bytes 2097168 | tf_op jit(solution)/shard_map/all_gather | solution.py:33
  233.0 3.1 convolution_convert_fusion.4
  236.2 1.2 copy.135
  237.4 1.2 copy.136
  238.8 17.0 %all_to_all.53 = f32[2,4,128,256]{2,3,0,1:T(8,128)S(1)} all-to-all(f32[2,4,128,256]{2,3,0,1:T(8,128)S(1)} %pad_maximum_fusion.1), channel_id=1, replica_groups=mesh['dp'=8,'mp'=4] {'mp'}, dimensions={1} | all-to-all | bytes 2097152 | tf_op jit(solution)/shard_map/all_to_all | solution.py:19
  255.9 1.0 copy.148
  257.1 4.8 %fusion.87 = (bf16[128,1024]{1,0:T(8,128)(2,1)}, f32[128,1024]{1,0:T(8,128)}) fusion(bf16[1024,1024]{0,1:T(8,128)(2,1)} %all-gather.11.cloned.1.call-done, bf16[1024,1024]{0,1:T(8,128)(2,1)} %all-gather.9.cloned.1.call-done, bf16[1024,1024]{0,1:T(8,128)(2,1)} %all-gather.7.cloned.1.call-done, s32[]{:T(128)S(6)} %select_n.28), kind=kOutput, calls=%fused_computation.120 | convolution fusion | flops 537133056 | bytes 5242884 | tf_op jit(solution)/shard_map/dot_general | solution.py:13
  261.9 3.1 convolution_convert_fusion.2
  265.1 3.5 all-to-all-start.7
  268.6 0.7 fusion.84
  269.3 0.7 iota_compare_fusion
  269.9 5.2 %all-to-all-done.7 = f32[8,1,256]{2,1,0:T(1,128)S(1)} async-done(((f32[8,1,256]{2,1,0:T(1,128)}), f32[8,1,256]{2,1,0:T(1,128)S(1)}, u32[]{:S(2)}, u32[]{:S(2)}) %all-to-all-start.7) | async-done | bytes 8224 | tf_op jit(solution)/shard_map/all_to_all | solution.py:114
  275.2 0.6 add_divide_fusion
  275.8 0.7 broadcast_select_fusion
  276.4 3.5 all-to-all-start.8
  279.9 3.1 all-gather.15.cloned.1.call-done
  283.1 2.1 fusion.2
  285.2 3.5 fusion.24
  288.9 43.8 %all-gather.13.cloned.1.call-done = bf16[1024,1024]{1,0:T(8,128)(2,1)} async-done(((bf16[128,1024]{1,0:T(8,128)(2,1)}), bf16[1024,1024]{1,0:T(8,128)(2,1)}) %all-gather.13.cloned.1.call-update) | async-done | bytes 2097168 | tf_op jit(solution)/shard_map/all_gather | solution.py:33
  332.7 2.1 fusion
  334.8 3.5 fusion.27
  338.5 44.4 %all-gather.17.cloned.1.call-done = bf16[1024,1024]{1,0:T(8,128)(2,1)} async-done(((bf16[128,1024]{1,0:T(8,128)(2,1)}), bf16[1024,1024]{1,0:T(8,128)(2,1)}) %all-gather.17.cloned.1.call-update) | async-done | bytes 2097168 | tf_op jit(solution)/shard_map/all_gather | solution.py:33
  382.9 2.1 convolution_convert_fusion.1
  385.3 1.0 pad_maximum_fusion.3
  386.3 3.6 all-to-all-start.5
  390.0 1.8 stack.88
  391.8 1.7 copy.124
  393.5 0.9 stack.90
  394.4 1.7 copy.126
  396.3 1.1 maximum_bitcast_fusion
  397.5 1.0 pad_maximum_fusion.2
  398.5 3.1 all-to-all-done.5
  401.6 4.2 all-to-all-start.3
  405.8 1.3 iota_compare_fusion.1
  407.0 1.4 iota_compare_fusion.3
  408.5 1.1 select_select_fusion
  409.5 7.9 %all-to-all-done.3 = bf16[4,3,1,128,256]{4,3,2,1,0:T(8,128)(2,1)} async-done(((bf16[4,3,1,128,256]{4,3,2,1,0:T(8,128)(2,1)}), bf16[4,3,1,128,256]{4,3,2,1,0:T(8,128)(2,1)}, u32[]{:S(2)}, u32[]{:S(2)}) %all-to-all-start.3) | async-done | bytes 786464 | tf_op jit(solution)/shard_map/all_to_all | solution.py:28
  417.4 3.5 all-to-all-start.6
  421.0 1.4 convert_bitcast_fusion
  422.7 1.5 fusion.48
  424.2 1.1 fusion.54
  425.3 10.1 %all-to-all-done.6 = bf16[8,128,256]{2,1,0:T(8,128)(2,1)S(1)} async-done(((bf16[8,128,256]{2,1,0:T(8,128)(2,1)}), bf16[8,128,256]{2,1,0:T(8,128)(2,1)S(1)}, u32[]{:S(2)}, u32[]{:S(2)}) %all-to-all-start.6) | async-done | bytes 524320 | tf_op jit(solution)/shard_map/all_to_all | solution.py:111
  435.3 0.8 copy.159
  436.1 0.6 copy.160
  (72 shorter events, 3.0 us)
Async XLA Ops:
  7.2 2.3 copy-start
  7.2 123.5 %all-gather.9.cloned.1.call-start = ((), (), s32[]{:S(2)}) async-start(), calls=%async_computation.10 | async-start | bytes 2359296 | tf_op jit(solution)/shard_map/all_gather | solution.py:33
  67.3 14.9 %copy-start.4 = (f32[4,128,256]{2,1,0:T(8,128)S(1)}, f32[4,128,256]{2,1,0:T(8,128)}, u32[]{:S(2)}) copy-start(f32[4,128,256]{2,1,0:T(8,128)} %param.19) | copy-start | bytes 1572868
  69.3 13.1 %copy-start.6 = (f32[4,128,256]{2,1,0:T(8,128)S(1)}, f32[4,128,256]{2,1,0:T(8,128)}, u32[]{:S(2)}) copy-start(f32[4,128,256]{2,1,0:T(8,128)} %param.18) | copy-start | bytes 1572868
  82.2 99.7 %all-gather.11.cloned.1.call-start = ((), (), s32[]{:S(2)}) async-start(), calls=%async_computation.11 | async-start | bytes 2359296 | tf_op jit(solution)/shard_map/all_gather | solution.py:33
  103.0 130.1 %all-gather.7.cloned.1.call-start = ((), (), s32[]{:S(2)}) async-start(), calls=%async_computation.9 | async-start | bytes 2359296 | tf_op jit(solution)/shard_map/all_gather | solution.py:33
  103.7 179.4 %all-gather.15.cloned.1.call-start = ((), (), s32[]{:S(2)}) async-start(), calls=%async_computation.13 | async-start | bytes 2359296 | tf_op jit(solution)/shard_map/all_gather | solution.py:33
  134.0 51.2 %copy-start.3 = (f32[1,128,4,256]{1,3,2,0:T(8,128)S(1)}, f32[1,128,4,256]{1,3,2,0:T(8,128)}, u32[]{:S(2)}) copy-start(f32[1,128,4,256]{1,3,2,0:T(8,128)} %get-tuple-element.17) | copy-start | bytes 1572868
  181.8 3.6 copy-start.1
  185.2 147.5 %all-gather.13.cloned.1.call-start = ((), (), s32[]{:S(2)}) async-start(), calls=%async_computation.12 | async-start | bytes 2359296 | tf_op jit(solution)/shard_map/all_gather | solution.py:33
  236.2 146.7 %all-gather.17.cloned.1.call-start = ((), (), s32[]{:S(2)}) async-start(), calls=%async_computation.14 | async-start | bytes 2359296 | tf_op jit(solution)/shard_map/all_gather | solution.py:33
  257.1 4.8 %copy-start.14 = (f32[128,1024]{1,0:T(8,128)S(1)}, f32[128,1024]{1,0:T(8,128)}, u32[]{:S(2)}) copy-start(f32[128,1024]{1,0:T(8,128)} %copy.148) | copy-start | bytes 1572868
  261.9 6.7 %copy-start.15 = (s32[5]{0:T(128)S(1)}, s32[5]{0:T(128)}, u32[]{:S(2)}) copy-start(s32[5]{0:T(128)} %param.15) | copy-start | bytes 64
  261.9 13.3 %copy-start.16 = (f32[256]{0:T(256)S(1)}, f32[256]{0:T(256)}, u32[]{:S(2)}) copy-start(f32[256]{0:T(256)} %param.23) | copy-start | bytes 3076
  261.9 13.3 %copy-start.17 = (f32[256]{0:T(256)S(1)}, f32[256]{0:T(256)}, u32[]{:S(2)}) copy-start(f32[256]{0:T(256)} %param.22) | copy-start | bytes 3076
  265.1 20.1 %copy-start.12 = (bf16[128,1024]{1,0:T(8,128)(2,1)S(1)}, bf16[128,1024]{1,0:T(8,128)(2,1)}, u32[]{:S(2)}) copy-start(bf16[128,1024]{1,0:T(8,128)(2,1)} %convolution_convert_fusion.3) | copy-start | bytes 786436
  265.1 10.1 %all-to-all-start.7 = ((f32[8,1,256]{2,1,0:T(1,128)}), f32[8,1,256]{2,1,0:T(1,128)S(1)}, u32[]{:S(2)}, u32[]{:S(2)}) async-start(f32[8,1,256]{2,1,0:T(1,128)} %bitcast.56), calls=%async_computation.7 | async-start | bytes 16384 | tf_op jit(solution)/shard_map/all_to_all | solution.py:114
  276.4 109.9 %all-to-all-start.8 = ((f32[8,1,256]{2,1,0:T(1,128)}), f32[8,1,256]{2,1,0:T(1,128)S(1)}, u32[]{:S(2)}, u32[]{:S(2)}) async-start(f32[8,1,256]{2,1,0:T(1,128)} %broadcast_select_fusion), calls=%async_computation.8 | async-start | bytes 16384 | tf_op jit(solution)/shard_map/all_to_all | solution.py:121
  288.6 46.1 %copy-start.13 = (bf16[128,1024]{1,0:T(8,128)(2,1)S(1)}, bf16[128,1024]{1,0:T(8,128)(2,1)}, u32[]{:S(2)}) copy-start(bf16[128,1024]{1,0:T(8,128)(2,1)} %convolution_convert_fusion.4) | copy-start | bytes 786436
  334.8 48.1 %copy-start.2 = (bf16[1,128,4,256]{1,3,2,0:T(8,128)(2,1)S(1)}, bf16[1,128,4,256]{1,3,2,0:T(8,128)(2,1)}, u32[]{:S(2)}) copy-start(bf16[1,128,4,256]{1,3,2,0:T(8,128)(2,1)} %get-tuple-element.21) | copy-start | bytes 786436
  385.3 8.2 %copy-start.10 = (bf16[128,1024]{1,0:T(8,128)(2,1)S(1)}, bf16[128,1024]{1,0:T(8,128)(2,1)}, u32[]{:S(2)}) copy-start(bf16[128,1024]{1,0:T(8,128)(2,1)} %get-tuple-element.42) | copy-start | bytes 786436
  386.3 9.7 %copy-start.11 = (bf16[128,1024]{1,0:T(8,128)(2,1)S(1)}, bf16[128,1024]{1,0:T(8,128)(2,1)}, u32[]{:S(2)}) copy-start(bf16[128,1024]{1,0:T(8,128)(2,1)} %get-tuple-element.44) | copy-start | bytes 786436
  386.3 15.2 %all-to-all-start.5 = ((bf16[4,3,1,128,256]{4,3,2,1,0:T(8,128)(2,1)}), bf16[4,3,1,128,256]{4,3,2,1,0:T(8,128)(2,1)S(1)}, u32[]{:S(2)}, u32[]{:S(2)}) async-start(bf16[4,3,1,128,256]{4,3,2,1,0:T(8,128)(2,1)} %pad_maximum_fusion.3), calls=%async_computation.5 | async-start | bytes 1572864 | tf_op jit(solution)/shard_map/all_to_all | solution.py:28
  401.6 15.9 %all-to-all-start.3 = ((bf16[4,3,1,128,256]{4,3,2,1,0:T(8,128)(2,1)}), bf16[4,3,1,128,256]{4,3,2,1,0:T(8,128)(2,1)}, u32[]{:S(2)}, u32[]{:S(2)}) async-start(bf16[4,3,1,128,256]{4,3,2,1,0:T(8,128)(2,1)} %pad_maximum_fusion.2), calls=%async_computation.3 | async-start | bytes 1572864 | tf_op jit(solution)/shard_map/all_to_all | solution.py:28
  417.4 17.9 %all-to-all-start.6 = ((bf16[8,128,256]{2,1,0:T(8,128)(2,1)}), bf16[8,128,256]{2,1,0:T(8,128)(2,1)S(1)}, u32[]{:S(2)}, u32[]{:S(2)}) async-start(bf16[8,128,256]{2,1,0:T(8,128)(2,1)} %select_select_fusion), calls=%async_computation.6 | async-start | bytes 1048576 | tf_op jit(solution)/shard_map/all_to_all | solution.py:111
  421.0 1.5 copy-start.5
  421.0 1.5 copy-start.7
  421.0 1.6 copy-start.8
  421.0 1.7 copy-start.9
Sparse Core Ops, SparseCore 0:
  82.3 48.3 all-gather.8
  133.3 48.5 all-gather.10
  184.5 48.5 all-gather.6
  235.6 47.4 all-gather.14
  285.0 47.5 all-gather.12
  335.2 47.6 all-gather.16
